TPU v7x, 32 devices: a whole 2x2x4 slice. The times are simulated.
32 devices in a mesh: pb: 8 (over z, core), ka: 4 (over y, x).
Axes of the slice: x: 2, y: 2, z: 4, core: 2. Of those that a mesh axis runs over, the one named last changes fastest.
Arguments:
- activations: bfloat16 [4, 1024, 768], P(None, ('pb', 'ka')), may hold values from -6 to 6
- attn_gain: float32 [768], replicated, may hold values from 0.1 to 1.9
- w_qkv: bfloat16 [768, 2304], replicated, may hold values from -0.21875 to 0.21875
- w_gate: bfloat16 [768, 768], replicated, may hold values from -0.21875 to 0.21875
- w_out: bfloat16 [768, 768], replicated, may hold values from -0.21875 to 0.21875
- pair_bias: bfloat16 [16, 1024, 1024], P(None, 'pb', 'ka'), may hold values from -240 to 240
- chain_ids: int32 [1024], replicated, may hold values from 0 to 5, as said below
- binder_flag: int32 [1024], replicated, may hold values from 0 to 1, as said below
- trans_gain: float32 [768], replicated, may hold values from 0.1 to 1.9
- w_up: bfloat16 [768, 3072], replicated, may hold values from -0.21875 to 0.21875
- w_down: bfloat16 [1536, 768], replicated, may hold values from -0.15625 to 0.15625
Outputs:
- updated: bfloat16 [4, 1024, 768], P(None, ('pb', 'ka'))
Inputs may be any that keep to these rules, and one draw needn't show every extreme that they name: `chain_ids`: chain ids never fall along the tokens; every chain has at least one token. `binder_flag`: all tokens of one chain carry the same flag.
All inputs are finite; a program needn't handle non-finite values.
Results may differ from a plain program's by a relative error of at most 0.0056.
Values may be sent and summed in bfloat16 or wider, within the bound.
No kernel may reach another device: no remote copies, remote signals or barrier semaphores. Data moves between devices by JAX's collectives and lax.ppermute only.
A program may use at most 128 MiB of HBM per device.

v0:
```python
import math

import jax
import jax.numpy as jnp
from jax import lax
from jax.sharding import PartitionSpec as P

epsilon = 1e-05
masked_score = -1000000000.0


def spread_2(value, axis, source):
    kept = jnp.where(lax.axis_index(axis) == source, value, 0).astype(value.dtype)
    return lax.psum(kept, axis)


def joined(value, axis, join):
    pieces = jax.tree.map(lambda part: lax.all_gather(part, axis), value)
    head = jax.tree.map(lambda part: part[0], pieces)
    tail = jax.tree.map(lambda part: part[1:], pieces)
    total, _ = lax.scan(lambda total, share: (join(total, share), None), head, tail)
    return total


def layer_norm(values, scales):
    centred = values - jnp.mean(values, axis=-1, keepdims=True)
    spread = jnp.mean(centred * centred, axis=-1, keepdims=True)
    return centred * lax.rsqrt(spread + epsilon) * scales


def block_stats(query_rows, key_block, value_block, bias_tile, allowed):
    head_count = bias_tile.shape[0]
    query_heads = query_rows.reshape(query_rows.shape[0], head_count, -1)
    key_heads = key_block.reshape(key_block.shape[0], head_count, -1)
    value_heads = value_block.reshape(value_block.shape[0], head_count, -1)
    head_size = query_heads.shape[-1]
    scores = jnp.einsum(
        "qhd,khd->hqk", query_heads, key_heads, preferred_element_type=jnp.float32
    ) / math.sqrt(head_size)
    scores = scores + bias_tile.astype(jnp.float32)
    best_score = jnp.max(jnp.where(allowed[None], scores, masked_score), axis=-1)
    weights = jnp.where(allowed[None], jnp.exp(scores - best_score[..., None]), 0.0)
    row_sum = jnp.sum(weights, axis=-1)
    block_out = jnp.einsum(
        "hqk,khd->qhd",
        weights.astype(jnp.bfloat16),
        value_heads,
        preferred_element_type=jnp.float32,
    )
    return (best_score.T, row_sum.T, block_out.reshape(query_rows.shape[0], -1))


def merge_pair(earlier, later):
    earlier_top, earlier_sum, earlier_out = earlier
    later_top, later_sum, later_out = later
    overall = jnp.maximum(earlier_top, later_top)
    earlier_factor = jnp.exp(earlier_top - overall)
    later_factor = jnp.exp(later_top - overall)
    row_sum = earlier_factor * earlier_sum + later_factor * later_sum
    shaped = earlier_out.shape[:-1] + (overall.shape[-1], -1)
    merged_out = earlier_factor[..., None] * earlier_out.reshape(shaped) + later_factor[
        ..., None
    ] * later_out.reshape(shaped)
    return (overall, row_sum, merged_out.reshape(earlier_out.shape))


def body(
    activations,
    attn_gain,
    w_qkv,
    w_gate,
    w_out,
    pair_bias,
    chain_ids,
    binder_flag,
    trans_gain,
    w_up,
    w_down,
):
    samples, own_rows, model_width = activations.shape
    head_count, query_count, key_count = pair_bias.shape
    pb_ratio = lax.axis_size("pb") // lax.axis_size("ka")
    normed = layer_norm(activations.astype(jnp.float32), attn_gain).astype(jnp.bfloat16)
    flat_normed = normed.reshape(-1, model_width)
    gate_pre = jnp.dot(flat_normed, w_gate, preferred_element_type=jnp.float32).reshape(
        samples, own_rows, model_width
    )
    queries = jnp.dot(flat_normed, w_qkv[:, :model_width], preferred_element_type=jnp.float32)
    queries = queries.astype(jnp.bfloat16).reshape(samples, own_rows, model_width)
    queries, block_normed = (
        lax.all_gather(queries, "ka", axis=1, tiled=True),
        lax.all_gather(normed, "ka", axis=1, tiled=True),
    )
    input_parts = []
    for within in range(pb_ratio):
        source_index = lax.axis_index("ka") * pb_ratio + within
        input_parts.append(spread_2(block_normed, "pb", source_index))
    key_inputs = jnp.concatenate(input_parts, axis=1).reshape(-1, model_width)
    key_value = jnp.dot(key_inputs, w_qkv[:, model_width:], preferred_element_type=jnp.float32)
    key_block = (
        key_value[:, :model_width].astype(jnp.bfloat16).reshape(samples, key_count, model_width)
    )
    value_block = (
        key_value[:, model_width:].astype(jnp.bfloat16).reshape(samples, key_count, model_width)
    )
    query_start = lax.axis_index("pb") * query_count
    key_start = lax.axis_index("ka") * key_count
    row_chain = lax.dynamic_slice_in_dim(chain_ids, query_start, query_count, 0)
    row_binder = lax.dynamic_slice_in_dim(binder_flag, query_start, query_count, 0)
    col_chain = lax.dynamic_slice_in_dim(chain_ids, key_start, key_count, 0)
    col_binder = lax.dynamic_slice_in_dim(binder_flag, key_start, key_count, 0)
    allowed = (
        (row_binder[:, None] > 0)
        | (col_binder[None, :] > 0)
        | (row_chain[:, None] == col_chain[None, :])
    )

    def per_sample(operands):
        return block_stats(operands[0], operands[1], operands[2], pair_bias, allowed)

    block_tops, block_sums, block_outs = lax.map(per_sample, (queries, key_block, value_block))
    block_tops, block_sums, block_outs = joined(
        (block_tops, block_sums, block_outs), "ka", merge_pair
    )
    offset = lax.axis_index("ka") * own_rows
    row_sum = lax.dynamic_slice_in_dim(block_sums, offset, own_rows, 1)
    row_out = lax.dynamic_slice_in_dim(block_outs, offset, own_rows, 1)
    attention = (row_out.reshape(samples, own_rows, head_count, -1) / row_sum[..., None]).reshape(
        samples, own_rows, model_width
    )
    gated = (jax.nn.sigmoid(gate_pre) * attention).astype(jnp.bfloat16)
    mixed = activations.astype(jnp.float32) + jnp.dot(
        gated.reshape(-1, model_width), w_out, preferred_element_type=jnp.float32
    ).reshape(samples, own_rows, model_width)
    trans_normed = layer_norm(mixed, trans_gain).astype(jnp.bfloat16)
    both_parts = jnp.dot(
        trans_normed.reshape(-1, model_width), w_up, preferred_element_type=jnp.float32
    )
    hidden_width = w_down.shape[0]
    hidden = (jax.nn.silu(both_parts[:, :hidden_width]) * both_parts[:, hidden_width:]).astype(
        jnp.bfloat16
    )
    updated = mixed + jnp.dot(hidden, w_down, preferred_element_type=jnp.float32).reshape(
        samples, own_rows, model_width
    )
    return updated.astype(jnp.bfloat16)


def solution(mesh):
    placed = (
        P(None, ("pb", "ka"), None),
        P(),
        P(),
        P(),
        P(),
        P(None, "pb", "ka"),
        P(),
        P(),
        P(),
        P(),
        P(),
    )
    return jax.shard_map(
        body, mesh=mesh, in_specs=placed, out_specs=P(None, ("pb", "ka"), None), check_vma=False
    )
```

profile of v0, /device:TPU:0, one launch (start us, length us, event | category | flops | bytes accessed | tf_op | source)
XLA Modules:
  0.0 271.9 jit_solution(7800680378099622818)
XLA Ops:
  10.0 12.7 %all_gather.25 = bf16[4,128,768]{2,1,0:T(8,128)(2,1)S(1)} all-gather(bf16[4,32,768]{2,1,0:T(8,128)(2,1)S(1)} %fusion.35), channel_id=1, replica_groups=mesh['pb'=8,'ka'=4] {'ka'}, dimensions={1}, use_global_device_ids=true | all-gather | bytes 983040 | tf_op jit(solution)/shard_map/all_gather | solution.py:92
  27.3 12.1 %all_gather.24 = bf16[4,128,768]{2,0,1:T(4,128)(2,1)S(1)} all-gather(bf16[4,32,768]{2,0,1:T(4,128)(2,1)S(1)} %copy.24), channel_id=1, replica_groups=mesh['pb'=8,'ka'=4] {'ka'}, dimensions={1}, use_global_device_ids=true | all-gather | bytes 983040 | tf_op jit(solution)/shard_map/all_gather | solution.py:91
  42.3 44.2 %all-reduce.3.cloned.1.call-done = (bf16[4,128,768]{2,1,0:T(8,128)(2,1)}, bf16[4,128,768]{2,1,0:T(8,128)(2,1)}) async-done(((bf16[4,128,768]{2,1,0:T(8,128)(2,1)}, bf16[4,128,768]{2,1,0:T(8,128)(2,1)}), (bf16[4,128,768]{2,1,0:T(8,128)(2,1)}, bf16[4,128,768]{2,1,0:T(8,128)(2,1)})) %all-reduce.3.cloned.1.call-update) | async-done | bytes 1572880 | tf_op jit(solution)/shard_map/psum | solution.py:14
  88.0 4.5 %convolution_convert_fusion = bf16[1024,1536]{1,0:T(8,128)(2,1)S(1)} fusion(bf16[1024,768]{1,0:T(8,128)(2,1)S(1)} %bitcast.100, bf16[768,2304]{1,0:T(8,128)(2,1)} %param.17), kind=kOutput, calls=%fused_computation.28 | convolution fusion | flops 2417491968 | bytes 7077888 | tf_op jit(solution)/shard_map/dot_general | solution.py:99
  94.4 50.9 %while.30 = (s32[]{:T(128)}, f32[4,128,16]{1,2,0:T(8,128)}, f32[4,128,16]{1,2,0:T(8,128)}, f32[4,128,768]{2,1,0:T(8,128)}, bf16[4,128,768]{1,2,0:T(8,128)(2,1)},...) while((s32[]{:T(128)}, f32[4,128,16]{1,2,0:T(8,128)}, ...), condition=%wide.region_7.8_spmd.clone, body=%wide.region_4.7_spmd.clone.sunk | while | flops 106524672 | bytes 14295217 | solution.py:121
  96.7 3.2 %select_reduce_fusion.2 = (f32[16,128]{1,0:T(8,128)S(1)}, f32[16,128,256]{2,1,0:T(8,128)}) fusion(pred[128,256]{1,0:T(8,128)(4,1)S(1)} %compare_or_fusion.2, bf16[16,128,256]{2,1,0:T(8,128)(2,1)} %get-tuple-element.395, bf16[128,16,48]{0,2,1:T(8,128)(2,1)S(1)} %bitcast.97, bf16[256,16,48]{0,2,1:T(8,128)(2,1)S(1)} %bitcast.93), kind=kOutput, calls=%fused_computation.12.clone.1 | convolution fusion | flops 52951040 | bytes 3776512 | tf_op jit(solution)/shard_map/while/body/eval_jaxpr/qhd,khd->hqk/dot_general | solution.py:37
  109.4 3.2 %select_reduce_fusion.2 = (f32[16,128]{1,0:T(8,128)S(1)}, f32[16,128,256]{2,1,0:T(8,128)}) fusion(pred[128,256]{1,0:T(8,128)(4,1)S(1)} %compare_or_fusion.2, bf16[16,128,256]{2,1,0:T(8,128)(2,1)} %get-tuple-element.395, bf16[128,16,48]{0,2,1:T(8,128)(2,1)S(1)} %bitcast.97, bf16[256,16,48]{0,2,1:T(8,128)(2,1)S(1)} %bitcast.93), kind=kOutput, calls=%fused_computation.12.clone.1 | convolution fusion | flops 52951040 | bytes 3776512 | tf_op jit(solution)/shard_map/while/body/eval_jaxpr/qhd,khd->hqk/dot_general | solution.py:37
  122.1 3.2 %select_reduce_fusion.2 = (f32[16,128]{1,0:T(8,128)S(1)}, f32[16,128,256]{2,1,0:T(8,128)}) fusion(pred[128,256]{1,0:T(8,128)(4,1)S(1)} %compare_or_fusion.2, bf16[16,128,256]{2,1,0:T(8,128)(2,1)} %get-tuple-element.395, bf16[128,16,48]{0,2,1:T(8,128)(2,1)S(1)} %bitcast.97, bf16[256,16,48]{0,2,1:T(8,128)(2,1)S(1)} %bitcast.93), kind=kOutput, calls=%fused_computation.12.clone.1 | convolution fusion | flops 52951040 | bytes 3776512 | tf_op jit(solution)/shard_map/while/body/eval_jaxpr/qhd,khd->hqk/dot_general | solution.py:37
  134.8 3.2 %select_reduce_fusion.2 = (f32[16,128]{1,0:T(8,128)S(1)}, f32[16,128,256]{2,1,0:T(8,128)}) fusion(pred[128,256]{1,0:T(8,128)(4,1)S(1)} %compare_or_fusion.2, bf16[16,128,256]{2,1,0:T(8,128)(2,1)} %get-tuple-element.395, bf16[128,16,48]{0,2,1:T(8,128)(2,1)S(1)} %bitcast.97, bf16[256,16,48]{0,2,1:T(8,128)(2,1)S(1)} %bitcast.93), kind=kOutput, calls=%fused_computation.12.clone.1 | convolution fusion | flops 52951040 | bytes 3776512 | tf_op jit(solution)/shard_map/while/body/eval_jaxpr/qhd,khd->hqk/dot_general | solution.py:37
  146.0 8.5 %all-gather = f32[16,128,16]{1,2,0:T(8,128)S(1)} all-gather(f32[4,128,16]{1,2,0:T(8,128)S(1)} %copy-done.3), channel_id=2, replica_groups=mesh['pb'=8,'ka'=4] {'ka'}, dimensions={0}, use_global_device_ids=true | all-gather | bytes 163840 | tf_op jit(solution)/shard_map/all_gather | solution.py:18
  154.5 9.6 %all-gather.1 = f32[16,128,16]{1,2,0:T(8,128)S(1)} all-gather(f32[4,128,16]{1,2,0:T(8,128)S(1)} %copy-done.4), channel_id=3, replica_groups=mesh['pb'=8,'ka'=4] {'ka'}, dimensions={0}, use_global_device_ids=true | all-gather | bytes 163840 | tf_op jit(solution)/shard_map/all_gather | solution.py:18
  164.2 51.0 %all-gather.5.cloned.1.call-done = f32[16,128,768]{2,1,0:T(8,128)} async-done(((f32[4,128,768]{2,1,0:T(8,128)}), f32[16,128,768]{2,1,0:T(8,128)}) %all-gather.5.cloned.1.call-update) | async-done | bytes 6291472 | tf_op jit(solution)/shard_map/all_gather | solution.py:18
  217.9 3.0 %copy.29 = f32[4,128,768]{1,2,0:T(8,128)} copy(f32[4,128,768]{2,1,0:T(8,128)} %slice.60) | data formatting | bytes 3145728 | tf_op jit(solution)/shard_map/while | solution.py:21
  220.9 4.9 %slice.63 = f32[12,128,768]{2,1,0:T(8,128)} slice(f32[16,128,768]{2,1,0:T(8,128)} %all-gather.5.cloned.1.call-done), slice={[4:16], [0:128], [0:768]} | slice | bytes 9437184 | tf_op jit(solution)/shard_map/slice | solution.py:20
  225.8 27.0 %while.29 = (s32[]{:T(128)}, f32[4,128,16]{1,2,0:T(8,128)S(1)}, f32[4,128,16]{1,2,0:T(8,128)S(1)}, f32[4,128,768]{1,2,0:T(8,128)}, f32[3,4,128,16]{2,3,1,0:T(8,1...) while((s32[]{:T(128)}, f32[4,128,16]{1,2,0:T(8,128)S(1)}, ...), condition=%wide.region_9.10_spmd, body=%wide.region_8.9_spmd.sunk | while | flops 1228802 | bytes 11337821 | solution.py:21
  225.8 2.7 constant_dynamic-slice_fusion.9
  228.6 3.0 %copy.46 = f32[1,4,128,768]{2,3,1,0:T(8,128)} copy(f32[1,4,128,768]{3,2,1,0:T(8,128)} %constant_dynamic-slice_fusion.9) | data formatting | bytes 3145728 | tf_op jit(solution)/shard_map/while/body/jit(dynamic_index_in_dim)/dynamic_slice | solution.py:21
  231.6 3.2 %fusion.72 = f32[4,128,768]{1,2,0:T(8,128)} fusion(f32[1,4,128,768]{2,3,1,0:T(8,128)} %copy.46, f32[4,128,768]{1,2,0:T(8,128)} %get-tuple-element.413, f32[4,128,16]{1,2,0:T(8,128)S(1)} %get-tuple-element.345, f32[4,128,16]{1,2,0:T(8,128)S(1)} %get-tuple-element.346), kind=kLoop, calls=%fused_computation.2.clone.1 | loop fusion | flops 1179648 | bytes 4784128 | tf_op jit(solution)/shard_map/while/body/eval_jaxpr/add | solution.py:61
  237.6 3.0 %copy.46 = f32[1,4,128,768]{2,3,1,0:T(8,128)} copy(f32[1,4,128,768]{3,2,1,0:T(8,128)} %constant_dynamic-slice_fusion.9) | data formatting | bytes 3145728 | tf_op jit(solution)/shard_map/while/body/jit(dynamic_index_in_dim)/dynamic_slice | solution.py:21
  240.6 3.2 %fusion.72 = f32[4,128,768]{1,2,0:T(8,128)} fusion(f32[1,4,128,768]{2,3,1,0:T(8,128)} %copy.46, f32[4,128,768]{1,2,0:T(8,128)} %get-tuple-element.413, f32[4,128,16]{1,2,0:T(8,128)S(1)} %get-tuple-element.345, f32[4,128,16]{1,2,0:T(8,128)S(1)} %get-tuple-element.346), kind=kLoop, calls=%fused_computation.2.clone.1 | loop fusion | flops 1179648 | bytes 4784128 | tf_op jit(solution)/shard_map/while/body/eval_jaxpr/add | solution.py:61
  246.6 3.0 %copy.46 = f32[1,4,128,768]{2,3,1,0:T(8,128)} copy(f32[1,4,128,768]{3,2,1,0:T(8,128)} %constant_dynamic-slice_fusion.9) | data formatting | bytes 3145728 | tf_op jit(solution)/shard_map/while/body/jit(dynamic_index_in_dim)/dynamic_slice | solution.py:21
  249.6 3.2 %fusion.72 = f32[4,128,768]{1,2,0:T(8,128)} fusion(f32[1,4,128,768]{2,3,1,0:T(8,128)} %copy.46, f32[4,128,768]{1,2,0:T(8,128)} %get-tuple-element.413, f32[4,128,16]{1,2,0:T(8,128)S(1)} %get-tuple-element.345, f32[4,128,16]{1,2,0:T(8,128)S(1)} %get-tuple-element.346), kind=kLoop, calls=%fused_computation.2.clone.1 | loop fusion | flops 1179648 | bytes 4784128 | tf_op jit(solution)/shard_map/while/body/eval_jaxpr/add | solution.py:61
  252.8 3.0 %copy.31 = f32[4,128,768]{2,1,0:T(8,128)} copy(f32[4,128,768]{1,2,0:T(8,128)} %get-tuple-element.95) | data formatting | bytes 3145728 | tf_op jit(solution)/shard_map/while | solution.py:21
  260.6 3.2 %fusion.54 = f32[128,3072]{1,0:T(8,128)S(1)} fusion(bf16[128,768]{1,0:T(8,128)(2,1)S(1)} %bitcast.101, bf16[768,3072]{1,0:T(8,128)(2,1)} %param.24), kind=kOutput, calls=%fused_computation.74 | convolution fusion | flops 603979776 | bytes 6488064 | tf_op jit(solution)/shard_map/dot_general | solution.py:136
  (153 shorter events, 67.1 us)
Async XLA Ops:
  6.5 257.2 %copy-start = (bf16[1536,768]{1,0:T(8,128)(2,1)S(1)}, bf16[1536,768]{1,0:T(8,128)(2,1)}, u32[]{:S(2)}) copy-start(bf16[1536,768]{1,0:T(8,128)(2,1)} %param.25) | copy-start | bytes 7077892
  6.5 80.0 %all-reduce.3.cloned.1.call-start = ((), (), s32[]{:S(2)}) async-start(), calls=%async_computation.1 | async-start | bytes 3145728 | tf_op jit(solution)/shard_map/psum | solution.py:14
  24.0 191.2 %all-gather.5.cloned.1.call-start = ((), (), s32[]{:S(2)}) async-start(), calls=%async_computation | async-start | bytes 7864320 | tf_op jit(solution)/shard_map/all_gather | solution.py:18
  94.4 5.5 %copy-start.7 = (s32[128]{0:T(128)}, s32[128]{0:T(128)S(1)}, u32[]{:S(2)}) copy-start(s32[128]{0:T(128)S(1)} %get-tuple-element.400) | copy-start | bytes 1540 | tf_op jit(solution)/shard_map/while
  94.4 5.5 %copy-start.9 = (pred[128]{0:T(512)(128)(4,1)}, pred[128]{0:T(512)(128)(4,1)S(1)}, u32[]{:S(2)}) copy-start(pred[128]{0:T(512)(128)(4,1)S(1)} %get-tuple-element.398) | copy-start | bytes 388 | tf_op jit(solution)/shard_map/while
  96.6 3.2 %copy-start.1 = (pred[128,256]{1,0:T(8,128)(4,1)}, pred[128,256]{1,0:T(8,128)(4,1)S(1)}, u32[]{:S(2)}) copy-start(pred[128,256]{1,0:T(8,128)(4,1)S(1)} %compare_or_fusion.2) | copy-start | bytes 98308 | tf_op jit(solution)/shard_map/while
  103.4 3.7 %copy-start.8 = (s32[128]{0:T(128)S(1)}, s32[128]{0:T(128)}, u32[]{:S(2)}) copy-start(s32[128]{0:T(128)} %copy-done.7) | copy-start | bytes 1540 | tf_op jit(solution)/shard_map/while
  103.4 3.7 %copy-start.10 = (pred[128]{0:T(512)(128)(4,1)S(1)}, pred[128]{0:T(512)(128)(4,1)}, u32[]{:S(2)}) copy-start(pred[128]{0:T(512)(128)(4,1)} %copy-done.9) | copy-start | bytes 388 | tf_op jit(solution)/shard_map/while
  107.1 5.5 %copy-start.7 = (s32[128]{0:T(128)}, s32[128]{0:T(128)S(1)}, u32[]{:S(2)}) copy-start(s32[128]{0:T(128)S(1)} %get-tuple-element.400) | copy-start | bytes 1540 | tf_op jit(solution)/shard_map/while
  107.1 5.5 %copy-start.9 = (pred[128]{0:T(512)(128)(4,1)}, pred[128]{0:T(512)(128)(4,1)S(1)}, u32[]{:S(2)}) copy-start(pred[128]{0:T(512)(128)(4,1)S(1)} %get-tuple-element.398) | copy-start | bytes 388 | tf_op jit(solution)/shard_map/while
  109.4 3.2 %copy-start.1 = (pred[128,256]{1,0:T(8,128)(4,1)}, pred[128,256]{1,0:T(8,128)(4,1)S(1)}, u32[]{:S(2)}) copy-start(pred[128,256]{1,0:T(8,128)(4,1)S(1)} %compare_or_fusion.2) | copy-start | bytes 98308 | tf_op jit(solution)/shard_map/while
  116.1 3.7 %copy-start.8 = (s32[128]{0:T(128)S(1)}, s32[128]{0:T(128)}, u32[]{:S(2)}) copy-start(s32[128]{0:T(128)} %copy-done.7) | copy-start | bytes 1540 | tf_op jit(solution)/shard_map/while
  116.1 3.7 %copy-start.10 = (pred[128]{0:T(512)(128)(4,1)S(1)}, pred[128]{0:T(512)(128)(4,1)}, u32[]{:S(2)}) copy-start(pred[128]{0:T(512)(128)(4,1)} %copy-done.9) | copy-start | bytes 388 | tf_op jit(solution)/shard_map/while
  119.8 5.5 %copy-start.7 = (s32[128]{0:T(128)}, s32[128]{0:T(128)S(1)}, u32[]{:S(2)}) copy-start(s32[128]{0:T(128)S(1)} %get-tuple-element.400) | copy-start | bytes 1540 | tf_op jit(solution)/shard_map/while
  119.8 5.5 %copy-start.9 = (pred[128]{0:T(512)(128)(4,1)}, pred[128]{0:T(512)(128)(4,1)S(1)}, u32[]{:S(2)}) copy-start(pred[128]{0:T(512)(128)(4,1)S(1)} %get-tuple-element.398) | copy-start | bytes 388 | tf_op jit(solution)/shard_map/while
  122.1 3.2 %copy-start.1 = (pred[128,256]{1,0:T(8,128)(4,1)}, pred[128,256]{1,0:T(8,128)(4,1)S(1)}, u32[]{:S(2)}) copy-start(pred[128,256]{1,0:T(8,128)(4,1)S(1)} %compare_or_fusion.2) | copy-start | bytes 98308 | tf_op jit(solution)/shard_map/while
  128.9 3.7 %copy-start.8 = (s32[128]{0:T(128)S(1)}, s32[128]{0:T(128)}, u32[]{:S(2)}) copy-start(s32[128]{0:T(128)} %copy-done.7) | copy-start | bytes 1540 | tf_op jit(solution)/shard_map/while
  128.9 3.7 %copy-start.10 = (pred[128]{0:T(512)(128)(4,1)S(1)}, pred[128]{0:T(512)(128)(4,1)}, u32[]{:S(2)}) copy-start(pred[128]{0:T(512)(128)(4,1)} %copy-done.9) | copy-start | bytes 388 | tf_op jit(solution)/shard_map/while
  132.5 5.5 %copy-start.7 = (s32[128]{0:T(128)}, s32[128]{0:T(128)S(1)}, u32[]{:S(2)}) copy-start(s32[128]{0:T(128)S(1)} %get-tuple-element.400) | copy-start | bytes 1540 | tf_op jit(solution)/shard_map/while
  132.5 5.5 %copy-start.9 = (pred[128]{0:T(512)(128)(4,1)}, pred[128]{0:T(512)(128)(4,1)S(1)}, u32[]{:S(2)}) copy-start(pred[128]{0:T(512)(128)(4,1)S(1)} %get-tuple-element.398) | copy-start | bytes 388 | tf_op jit(solution)/shard_map/while
  134.8 3.2 %copy-start.1 = (pred[128,256]{1,0:T(8,128)(4,1)}, pred[128,256]{1,0:T(8,128)(4,1)S(1)}, u32[]{:S(2)}) copy-start(pred[128,256]{1,0:T(8,128)(4,1)S(1)} %compare_or_fusion.2) | copy-start | bytes 98308 | tf_op jit(solution)/shard_map/while
  141.6 3.7 %copy-start.8 = (s32[128]{0:T(128)S(1)}, s32[128]{0:T(128)}, u32[]{:S(2)}) copy-start(s32[128]{0:T(128)} %copy-done.7) | copy-start | bytes 1540 | tf_op jit(solution)/shard_map/while
  141.6 3.7 %copy-start.10 = (pred[128]{0:T(512)(128)(4,1)S(1)}, pred[128]{0:T(512)(128)(4,1)}, u32[]{:S(2)}) copy-start(pred[128]{0:T(512)(128)(4,1)} %copy-done.9) | copy-start | bytes 388 | tf_op jit(solution)/shard_map/while
  145.3 9.2 %copy-start.4 = (f32[4,128,16]{1,2,0:T(8,128)S(1)}, f32[4,128,16]{1,2,0:T(8,128)}, u32[]{:S(2)}) copy-start(f32[4,128,16]{1,2,0:T(8,128)} %get-tuple-element.93) | copy-start | bytes 98308
  (11 other events, 15.0 us)
Sparse Core Ops, SparseCore 0:
  24.1 62.3 all-reduce.2
  145.4 69.6 all-gather.4
where the time goes:
time: 274 us; the launch traced here: 272 us
  waiting for transfers between devices  95.2 us (35%)
  local copies, waits for them, and re-layouts  58 us (21%)
  blocking collectives  42.9 us (16%)
  matrix products  33.9 us (12%)
  other arithmetic  27.9 us (10%)
  between operations  13.6 us (5%)
    all_gather x1, waiting for transfers between devices, joined(): pieces = jax.tree.map(lambda part: lax.all_gather(part, axis), value)  51 us
    psum x1, waiting for transfers between devices, spread_2(): return lax.psum(kept, axis)  44.2 us
    all_gather x2, blocking collectives, joined(): pieces = jax.tree.map(lambda part: lax.all_gather(part, axis), value)  18.1 us
    dynamic_slice x6, local copies, waits for them, and re-layouts, joined(): lax.scan(lambda total, share: (join(total, share), None), head, tail)  17.2 us
    dynamic_slice x20, local copies, waits for them, and re-layouts, body(): lax.map(per_sample, (queries, key_block, value_block))  13.4 us
    dot_general x4, matrix products, block_stats(): jnp.einsum('qhd,khd->hqk', query_heads, key_heads, preferred_element_type...  12.7 us
    all_gather x1, blocking collectives, body(): lax.all_gather(normed, 'ka', axis=1, tiled=True)  12.7 us
    all_gather x1, blocking collectives, body(): lax.all_gather(queries, 'ka', axis=1, tiled=True)  12.1 us
  transfers between devices with their start and end apart: 2, of which 2 were waited for; matrix products, arithmetic and copies ran while one was open for 2% of the time, Pallas kernels for 0%

commit v1 on v0

v1 whole, which is shorter than its diff:
```python
import functools
import math

import jax
import jax.numpy as jnp
from jax import lax
from jax.experimental import pallas as pl
from jax.experimental.pallas import tpu as pltpu
from jax.sharding import PartitionSpec as P

epsilon = 1e-05
masked_score = -1500000000.0
log2e = math.log2(math.e)
lanes = 128
window = 256
f32 = jnp.float32
bf16 = jnp.bfloat16
nt = (((1,), (1,)), ((), ()))
tn = (((0,), (0,)), ((), ()))


def whole():
    return pl.BlockSpec(memory_space=pltpu.VMEM)


def cost(flops, moved):
    return pl.CostEstimate(flops=int(flops), bytes_accessed=int(moved), transcendentals=0)


def partner(i, step, n):
    return i ^ step if n & (n - 1) == 0 else (step - i) % n


def layer_norm(values, scales):
    centred = values - jnp.mean(values, axis=-1, keepdims=True)
    spread = jnp.mean(centred * centred, axis=-1, keepdims=True)
    return centred * lax.rsqrt(spread + epsilon) * scales


def norm_kernel(x_ref, gain_ref, out_ref):
    out_ref[...] = layer_norm(x_ref[...].astype(f32), gain_ref[...]).astype(bf16)


def gate_kernel(x_ref, w_ref, out_ref):
    gate = jnp.dot(x_ref[...], w_ref[...], preferred_element_type=f32)
    out_ref[...] = jax.nn.sigmoid(gate).T


def pair_start(first, size, width):
    span = min(window, width)
    return min(first * size // lanes * lanes, width - span)


def query_kernel(heads, scale, *refs):
    *piece_refs, w_ref, out_ref = refs
    samples, rows, width = piece_refs[0].shape
    size = width // heads
    count = len(piece_refs) * rows
    span = out_ref.shape[-1]
    column = lax.broadcasted_iota(jnp.int32, (samples * rows, span), 1)
    for at, piece in enumerate(piece_refs):
        flat = piece[...].reshape(samples * rows, width)
        made = jnp.dot(flat, w_ref[...], preferred_element_type=f32) * scale
        for head in range(heads):
            start = pair_start(head // 2 * 2, size, width)
            kept = (column >= head * size - start) & (column < (head + 1) * size - start)
            picked = jnp.where(kept, made[:, start : start + span], 0.0).astype(bf16)
            spot = head % 2 * count + at * rows
            out_ref[:, head // 2, spot : spot + rows, :] = picked.reshape(samples, rows, span)


def bias_kernel(n, rows, place_ref, row_ref, col_ref, bias_ref, out_ref, turned, flipped):
    query_count, key_count = bias_ref.shape[1:]
    group, core, ka = place_ref[0], place_ref[1], place_ref[2]
    cores = key_count // query_count
    row_code, col_code = row_ref[...], col_ref[...]
    allowed = (row_code < 0) | (col_code < 0) | (row_code == col_code)
    turned[...] = jnp.where(allowed, bias_ref[0].astype(f32) * log2e, masked_score)
    ordered = [
        turned[pl.ds(pl.multiple_of(partner(ka, step, n) * rows, rows), rows), :]
        for step in range(n)
    ]
    flipped[...] = jnp.concatenate(ordered, axis=0).T
    for shift in range(cores):
        for step in range(n):
            source = lax.rem(core + cores - shift, cores) * query_count
            source = pl.multiple_of(source + partner(group, step, n) * rows, rows)
            spot = (shift * n + step) * rows
            out_ref[0, spot : spot + rows, :] = flipped[pl.ds(source, rows), :]


def attention_kernel(heads, *refs):
    (*piece_refs, q_ref, wk_ref, wv_ref, bias_ref, out_ref, x_buf, k_buf, v_buf) = refs
    rows, width = piece_refs[0].shape[1:]
    size = width // heads
    query_count = q_ref.shape[2] // 2
    sample = pl.program_id(0)
    for at, piece in enumerate(piece_refs):
        x_buf[at * rows : (at + 1) * rows, :] = piece[0]
    k_buf[...] = jnp.dot(x_buf[...], wk_ref[...], preferred_element_type=f32).astype(bf16)
    v_buf[...] = lax.dot_general(wv_ref[...], x_buf[...], nt, preferred_element_type=f32).astype(
        bf16
    )
    spot = sample * rows
    tile = pl.multiple_of(spot // lanes * lanes, lanes)
    within = spot % lanes
    lane = lax.broadcasted_iota(jnp.int32, (size, lanes), 1)
    mine = (lane >= within) & (lane < within + rows)
    lane_one = lax.broadcasted_iota(jnp.int32, (heads, lanes), 1)
    mine_one = (lane_one >= within) & (lane_one < within + rows)

    def put(values, first, count, mask):
        for at in range(query_count // rows):
            source = at * rows // lanes * lanes
            turn = lax.rem(within + lanes - at * rows % lanes, lanes)
            moved = pltpu.roll(values[:, source : source + lanes], turn, 1)
            spot = (at, slice(first, first + count), pl.ds(tile, lanes))
            out_ref[spot] = jnp.where(mask, moved, out_ref[spot].astype(f32)).astype(bf16)

    tops, sums = [], []
    span = q_ref.shape[-1]
    for first in range(0, heads, 2):
        start = pair_start(first, size, width)
        scores = lax.dot_general(
            k_buf[:, start : start + span],
            q_ref[0, first // 2],
            nt,
            preferred_element_type=f32,
        )
        for at in range(2):
            head = first + at
            score = scores[:, at * query_count : (at + 1) * query_count] + bias_ref[head]
            top = jnp.max(score, axis=0, keepdims=True)
            weight = jnp.exp2(score - top)
            total = jnp.sum(weight, axis=0, keepdims=True)
            made = jnp.dot(
                v_buf[head * size : (head + 1) * size, :],
                weight.astype(bf16),
                preferred_element_type=f32,
            )
            put(made * (1.0 / total), head * size, size, mine)
            tops.append(top)
            sums.append(total)
    level = jnp.concatenate(tops, axis=0) + jnp.log2(jnp.concatenate(sums, axis=0))
    for part in range(3):
        rounded = level.astype(bf16).astype(f32)
        put(rounded, width + part * heads, heads, mine_one)
        level = level - rounded


def finish_kernel(heads, *refs):
    *part_refs, gate_ref, act_ref, wo_ref, gain_ref, up_ref, down_ref, out_ref = refs
    width = act_ref.shape[-1]
    size = width // heads
    levels = []
    for part in part_refs:
        tail = part[width : width + 3 * heads, :].astype(f32)
        levels.append(tail[:heads] + (tail[heads : 2 * heads] + tail[2 * heads :]))
    best = functools.reduce(jnp.maximum, levels)
    shares = [jnp.exp2(level - best) for level in levels]
    inverse = 1.0 / functools.reduce(jnp.add, shares)
    shares = [share * inverse for share in shares]
    blocks = []
    for head in range(heads):
        where = slice(head * size, (head + 1) * size)
        merged = functools.reduce(
            jnp.add,
            [
                share[head : head + 1] * part[where, :].astype(f32)
                for share, part in zip(shares, part_refs)
            ],
        )
        blocks.append(merged * gate_ref[where, :])
    gated = jnp.concatenate(blocks, axis=0).T.astype(bf16)
    mixed = act_ref[...].astype(f32) + jnp.dot(gated, wo_ref[...], preferred_element_type=f32)
    normed = layer_norm(mixed, gain_ref[...]).astype(bf16)
    both = jnp.dot(normed, up_ref[...], preferred_element_type=f32)
    hidden = both.shape[1] // 2
    left = both[:, :hidden]
    made = (left / (1.0 + jnp.exp(-left)) * both[:, hidden:]).astype(bf16)
    out_ref[...] = (mixed + jnp.dot(made, down_ref[...], preferred_element_type=f32)).astype(bf16)


def body(
    activations,
    attn_gain,
    w_qkv,
    w_gate,
    w_out,
    pair_bias,
    chain_ids,
    binder_flag,
    trans_gain,
    w_up,
    w_down,
):
    samples, rows, width = activations.shape
    heads, query_count, key_count = pair_bias.shape
    n = lax.axis_size("ka")
    cores = lax.axis_size("pb") // n
    flat_rows = samples * rows
    pb, ka = lax.axis_index("pb"), lax.axis_index("ka")
    group, core = pb // cores, pb % cores

    normed = pl.pallas_call(
        norm_kernel,
        out_shape=jax.ShapeDtypeStruct((flat_rows, width), bf16),
        in_specs=[whole(), whole()],
        out_specs=whole(),
        name="norm",
        cost_estimate=cost(10 * flat_rows * width, 4 * flat_rows * width),
    )(activations.reshape(flat_rows, width), attn_gain.reshape(1, width))
    own = normed.reshape(samples, rows, width)

    def spread(value, step):
        pairs = []
        for g in range(n):
            for c in range(cores):
                for j in range(n):
                    target = (partner(j, step, n) * cores + c) * n + g
                    pairs.append(((g * cores + c) * n + j, target))
        return lax.ppermute(value, ("pb", "ka"), pairs)

    def swap(value, step):
        pairs = [
            (g * cores + c, g * cores + (c + step) % cores)
            for g in range(n)
            for c in range(cores)
        ]
        return lax.ppermute(value, "pb", pairs)

    def exchange(value, step):
        pairs = [(j, partner(j, step, n)) for j in range(n)]
        if all(a == b for a, b in pairs):
            return value
        return lax.ppermute(value, "ka", pairs)

    key_pieces = [spread(own, step) for step in range(n)]
    query_pieces = [exchange(own, step) for step in range(n)]
    for step in range(1, cores):
        key_pieces = key_pieces + [swap(piece, step) for piece in key_pieces[:n]]

    gate = pl.pallas_call(
        gate_kernel,
        out_shape=jax.ShapeDtypeStruct((width, flat_rows), f32),
        in_specs=[whole(), whole()],
        out_specs=whole(),
        name="gate",
        cost_estimate=cost(2 * flat_rows * width * width, 2 * width * width),
    )(normed, w_gate)

    code = jnp.where(binder_flag > 0, -1, chain_ids).astype(jnp.int32)
    row_code = lax.dynamic_slice_in_dim(code, pb * query_count, query_count, 0)
    col_code = lax.dynamic_slice_in_dim(code, ka * key_count, key_count, 0)
    place = jnp.stack([group, core, ka]).astype(jnp.int32)
    bias = pl.pallas_call(
        functools.partial(bias_kernel, n, rows),
        grid_spec=pltpu.PrefetchScalarGridSpec(
            num_scalar_prefetch=1,
            grid=(heads,),
            in_specs=[
                pl.BlockSpec((query_count, 1), lambda h, place: (0, 0)),
                pl.BlockSpec((1, key_count), lambda h, place: (0, 0)),
                pl.BlockSpec((1, query_count, key_count), lambda h, place: (h, 0, 0)),
            ],
            out_specs=pl.BlockSpec((1, key_count, query_count), lambda h, place: (h, 0, 0)),
            scratch_shapes=[
                pltpu.VMEM((query_count, key_count), f32),
                pltpu.VMEM((key_count, query_count), f32),
            ],
        ),
        out_shape=jax.ShapeDtypeStruct((heads, key_count, query_count), f32),
        name="bias",
        cost_estimate=cost(
            8 * heads * key_count * query_count, 6 * heads * key_count * query_count
        ),
    )(place, row_code.reshape(-1, 1), col_code.reshape(1, -1), pair_bias)

    size = width // heads
    span = min(window, width)
    masked = (samples, heads // 2, 2 * query_count, span)
    queries = pl.pallas_call(
        functools.partial(query_kernel, heads, log2e / math.sqrt(size)),
        grid=(1,),
        out_shape=jax.ShapeDtypeStruct(masked, bf16),
        in_specs=[pl.BlockSpec((samples, rows, width), lambda i: (0, 0, 0))] * n
        + [pl.BlockSpec((width, width), lambda i: (0, 0))],
        out_specs=pl.BlockSpec(masked, lambda i: (0, 0, 0, 0)),
        name="queries",
        cost_estimate=cost(
            2 * n * flat_rows * width * width, 2 * width * width + 2 * math.prod(masked)
        ),
    )(*query_pieces, w_qkv)

    value_weights = w_qkv[:, 2 * width :].T
    depth = width + 3 * heads
    once = dict(pipeline_mode=pl.Buffered(1))
    message = (n, depth, flat_rows)
    parts = pl.pallas_call(
        functools.partial(attention_kernel, heads),
        grid=(samples,),
        out_shape=jax.ShapeDtypeStruct(message, bf16),
        in_specs=[pl.BlockSpec((1, rows, width), lambda s: (s, 0, 0))] * (cores * n)
        + [
            pl.BlockSpec((1,) + masked[1:], lambda s: (s, 0, 0, 0)),
            pl.BlockSpec((width, width), lambda s: (0, 1), **once),
            pl.BlockSpec((width, width), lambda s: (0, 0), **once),
            pl.BlockSpec((heads, key_count, query_count), lambda s: (0, 0, 0), **once),
        ],
        out_specs=pl.BlockSpec(message, lambda s: (0, 0, 0)),
        scratch_shapes=[
            pltpu.VMEM((key_count, width), bf16),
            pltpu.VMEM((key_count, width), bf16),
            pltpu.VMEM((width, key_count), bf16),
        ],
        name="attention",
        cost_estimate=cost(
            4 * samples * key_count * width * width, 4 * heads * key_count * query_count
        ),
    )(*key_pieces, queries, w_qkv, value_weights, bias)
    parts = [exchange(parts[step], step) for step in range(n)]

    updated = pl.pallas_call(
        functools.partial(finish_kernel, heads),
        out_shape=jax.ShapeDtypeStruct((flat_rows, width), bf16),
        in_specs=[whole()] * (n + 6),
        out_specs=whole(),
        name="finish",
        cost_estimate=cost(
            2 * flat_rows * width * width * 7, 14 * width * width
        ),
    )(
        *parts,
        gate,
        activations.reshape(flat_rows, width),
        w_out,
        trans_gain.reshape(1, width),
        w_up,
        w_down,
    )
    return updated.reshape(samples, rows, width)


def solution(mesh):
    placed = (
        P(None, ("pb", "ka"), None),
        P(),
        P(),
        P(),
        P(),
        P(None, "pb", "ka"),
        P(),
        P(),
        P(),
        P(),
        P(),
    )
    return jax.shard_map(
        body, mesh=mesh, in_specs=placed, out_specs=P(None, ("pb", "ka"), None), check_vma=False
    )
```

time: 274 us -> 94 us (0.34)
  waiting for transfers between devices: 95.2 us -> 15.5 us
  local copies, waits for them, and re-layouts: 58 us -> 9.08 us
  blocking collectives: 42.9 us -> 0 us
  Pallas kernels: 0 us -> 39.4 us
  matrix products: 33.9 us -> 0 us
  starting transfers between devices: 0.04 us -> 27.6 us
  other arithmetic: 27.9 us -> 1.35 us
  between operations: 13.6 us -> 0.16 us
    all_gather x1 -> x0, waiting for transfers between devices: 51 us -> none  [joined(): pieces = jax.tree.map(lambda part: lax.all_gather(part, axis), value)]
    psum x1 -> x0, waiting for transfers between devices: 44.2 us -> none  [spread_2(): return lax.psum(kept, axis)]
    all_gather x4 -> x0, blocking collectives: 42.9 us -> none  [the longest x2 18.1 us: joined(): pieces = jax.tree.map(lambda part: lax.all_gather(part, axis), value)]
    pallas_call x0 -> x6, Pallas kernels: none -> 39.4 us  [the longest x1 12.9 us: body(): pl.pallas_call(functools.partial(attention_kernel, heads), grid=(samples,...]
    dot_general x13 -> x0, matrix products: 33.9 us -> none  [the longest x4 12.7 us: block_stats(): jnp.einsum('qhd,khd->hqk', query_heads, key_heads, preferred_element_type...]
    dynamic_slice x30 -> x1, local copies, waits for them, and re-layouts: 32.3 us -> 0.65 us  [body(): col_code = lax.dynamic_slice_in_dim(code, ka * key_count, key_count, 0)]
    ppermute x0 -> x14, starting transfers between devices: none -> 27.6 us  [the longest x6 15.2 us: exchange(): return lax.ppermute(value, 'ka', pairs)]
    ppermute x0 -> x14, waiting for transfers between devices: none -> 15.5 us  [the longest x6 15.5 us: exchange(): return lax.ppermute(value, 'ka', pairs)]
  transfers between devices with their start and end apart: 2 -> 14, of which waited for: 2 -> 4; matrix products, arithmetic and copies ran while one was open for 2% -> 5% of each run, Pallas kernels for 0% -> 19%
where the time goes in v1:
time: 94 us; the launch traced here: 93.1 us
  Pallas kernels  39.4 us (42%)
  starting transfers between devices  27.6 us (29%)
  waiting for transfers between devices  15.5 us (16%)
  local copies, waits for them, and re-layouts  9.08 us (10%)
  other arithmetic  1.35 us (1%)
    ppermute x6, waiting for transfers between devices, exchange(): return lax.ppermute(value, 'ka', pairs)  15.5 us
    ppermute x6, starting transfers between devices, exchange(): return lax.ppermute(value, 'ka', pairs)  15.2 us
    pallas_call x1, Pallas kernels, body(): pl.pallas_call(functools.partial(attention_kernel, heads), grid=(samples,...  12.9 us
    ppermute x4, starting transfers between devices, spread(): return lax.ppermute(value, ('pb', 'ka'), pairs)  11.8 us
    pallas_call x1, Pallas kernels, body(): pl.pallas_call(functools.partial(bias_kernel, n, rows), grid_spec=pltpu.P...  11.1 us
    pallas_call x1, Pallas kernels, body(): pl.pallas_call(functools.partial(finish_kernel, heads), out_shape=jax.Sha...  6.51 us
    pallas_call x1, Pallas kernels, body(): pl.pallas_call(functools.partial(query_kernel, heads, log2e / math.sqrt(s...  4.47 us
    unnamed x31, local copies, waits for them, and re-layouts  3.66 us
  transfers between devices with their start and end apart: 14, of which 4 were waited for; matrix products, arithmetic and copies ran while one was open for 5% of the time, Pallas kernels for 19%

profile of v1, /device:TPU:0, one launch (start us, length us, event | category | flops | bytes accessed | tf_op | source)
XLA Modules:
  0.0 93.1 jit_solution(16815447710448606894)
XLA Ops:
  0.0 1.4 %reshape.23.gain_ref = f32[1,768]{1,0:T(1,128)} reshape(f32[768]{0:T(1024)} %param.12) | data formatting | bytes 6144 | tf_op jit(solution)/shard_map/reshape | solution.py:212
  1.4 1.8 %norm.1.x_ref = bf16[128,768]{1,0:T(8,128)(2,1)} custom-call(bf16[128,768]{1,0:T(8,128)(2,1)} %bitcast.27, f32[1,768]{1,0:T(1,128)} %reshape.23.gain_ref), custom_call_target="tpu_custom_call" | custom-call | flops 983040 | bytes 393216 | tf_op jit(solution)/shard_map/norm/pallas_call | solution.py:205
  3.2 1.6 %collective-permute-start = (bf16[4,32,768]{2,1,0:T(8,128)(2,1)}, bf16[4,32,768]{2,1,0:T(8,128)(2,1)S(1)}, u32[]{:S(2)}, u32[]{:S(2)}) collective-permute-start(bf16[4,32,768]{2,1,0:T(8,128)(2,1)} %bitcast.19), channel_id=1, source_target_pairs={{0,0},{1,8},{2,16},{3,24},{4,4},{5,12},{6,20},{7,28},{8,1},{9,9},{... | collective-permute-start | bytes 589832 | tf_op jit(solution)/shard_map/ppermute | solution.py:222
  4.8 4.8 %collective-permute-start.1 = (bf16[4,32,768]{2,1,0:T(8,128)(2,1)}, bf16[4,32,768]{2,1,0:T(8,128)(2,1)S(1)}, u32[]{:S(2)}, u32[]{:S(2)}) collective-permute-start(bf16[4,32,768]{2,1,0:T(8,128)(2,1)} %bitcast.20), channel_id=1, source_target_pairs={{0,8},{1,0},{2,24},{3,16},{4,12},{5,4},{6,28},{7,20},{8,9},{9,1},{... | collective-permute-start | bytes 589832 | tf_op jit(solution)/shard_map/ppermute | solution.py:222
  9.6 3.5 %collective-permute-start.2 = (bf16[4,32,768]{2,1,0:T(8,128)(2,1)}, bf16[4,32,768]{2,1,0:T(8,128)(2,1)S(1)}, u32[]{:S(2)}, u32[]{:S(2)}) collective-permute-start(bf16[4,32,768]{2,1,0:T(8,128)(2,1)} %bitcast.21), channel_id=1, source_target_pairs={{0,16},{1,24},{2,0},{3,8},{4,20},{5,28},{6,4},{7,12},{8,17},{9,25}... | collective-permute-start | bytes 589832 | tf_op jit(solution)/shard_map/ppermute | solution.py:222
  13.1 1.9 %collective-permute-start.3 = (bf16[4,32,768]{2,1,0:T(8,128)(2,1)}, bf16[4,32,768]{2,1,0:T(8,128)(2,1)S(1)}, u32[]{:S(2)}, u32[]{:S(2)}) collective-permute-start(bf16[4,32,768]{2,1,0:T(8,128)(2,1)} %bitcast.22), channel_id=1, source_target_pairs={{0,24},{1,16},{2,8},{3,0},{4,28},{5,20},{6,12},{7,4},{8,25},{9,17}... | collective-permute-start | bytes 589832 | tf_op jit(solution)/shard_map/ppermute | solution.py:222
  15.0 1.5 %collective-permute-start.8 = (bf16[4,32,768]{2,1,0:T(8,128)(2,1)}, bf16[4,32,768]{2,1,0:T(8,128)(2,1)S(1)}, u32[]{:S(2)}, u32[]{:S(2)}) collective-permute-start(bf16[4,32,768]{2,1,0:T(8,128)(2,1)} %bitcast.23), channel_id=1, source_target_pairs={{0,1},{1,0},{2,3},{3,2},{4,5},{5,4},{6,7},{7,6},{8,9},{9,8},{10,11... | collective-permute-start | bytes 589832 | tf_op jit(solution)/shard_map/ppermute | solution.py:236
  16.5 9.8 %collective-permute-start.9 = (bf16[4,32,768]{2,1,0:T(8,128)(2,1)}, bf16[4,32,768]{2,1,0:T(8,128)(2,1)S(1)}, u32[]{:S(2)}, u32[]{:S(2)}) collective-permute-start(bf16[4,32,768]{2,1,0:T(8,128)(2,1)} %bitcast.24), channel_id=1, source_target_pairs={{0,2},{1,3},{2,0},{3,1},{4,6},{5,7},{6,4},{7,5},{8,10},{9,11},{10,... | collective-permute-start | bytes 589832 | tf_op jit(solution)/shard_map/ppermute | solution.py:236
  26.3 0.7 compare_select_fusion
  27.8 8.6 %collective-permute-done.9.refs_2_ = bf16[4,32,768]{2,1,0:T(8,128)(2,1)S(1)} collective-permute-done((bf16[4,32,768]{2,1,0:T(8,128)(2,1)}, bf16[4,32,768]{2,1,0:T(8,128)(2,1)S(1)}, u32[]{:S(2)}, u32[]{:S(2)}) %collective-permute-start.9) | collective-permute-done | bytes 196640 | tf_op jit(solution)/shard_map/ppermute | solution.py:236
  36.5 1.4 %copy.14 = bf16[768,768]{0,1:T(8,128)(2,1)} copy(bf16[768,768]{1,0:T(8,128)(2,1)S(1)} %slice-done) | data formatting | bytes 2359296
  37.9 0.7 copy.13.row_ref
  40.0 11.1 %bias.1.refs_11_ = f32[16,256,128]{2,1,0:T(8,128)} custom-call(s32[3]{0:T(128)} %pad_add_fusion.place_ref, s32[128,1]{1,0:T(8,128)} %copy.13.row_ref, s32[1,256]{1,0:T(1,128)} %bitcast.29, bf16[16,128,256]{2,1,0:T(8,128)(2,1)} %bias_ref.1), custom_call_target="tpu_custom_call" | custom-call | flops 4194304 | bytes 3145728 | tf_op jit(solution)/shard_map/bias/pallas_call | solution.py:256
  51.0 0.7 copy-done.11
  51.7 4.5 %queries.1.refs_8_ = bf16[4,8,256,256]{3,2,1,0:T(8,128)(2,1)} custom-call(bf16[4,32,768]{2,1,0:T(8,128)(2,1)} %bitcast.26, bf16[4,32,768]{2,1,0:T(8,128)(2,1)} %copy-done.7, bf16[4,32,768]{2,1,0:T(8,128)(2,1)} %copy-done.9, bf16[4,32,768]{2,1,0:T(8,128)(2,1)} %copy-done.11, bf16[768,2304]{1,0:T(8,128)(2,1)} %refs_9_.2), custom_call_target="tpu_custom_call" | custom-call | flops 603979776 | bytes 5373952 | tf_op jit(solution)/shard_map/queries/pallas_call | solution.py:282
  57.1 12.9 %attention.1 = bf16[4,816,128]{2,1,0:T(8,128)(2,1)} custom-call(bf16[4,32,768]{2,1,0:T(8,128)(2,1)} %copy-done.3, bf16[4,32,768]{2,1,0:T(8,128)(2,1)} %copy-done.4, bf16[4,32,768]{2,1,0:T(8,128)(2,1)} %copy-done.5, bf16[4,32,768]{2,1,0:T(8,128)(2,1)} %copy-done.6, bf16[4,32,768]{2,1,0:T(8,128)(2,1)} %copy-done.8, bf16[4,32,768]{2,1,0:T(8,128)(2,1)} %copy-done.10, ...), custom_call_target="tpu_custom_call" | custom-call | flops 2415919104 | bytes 2097152 | tf_op jit(solution)/shard_map/attention/pallas_call | solution.py:299
  70.0 2.0 %slice_bitcast_fusion = (bf16[816,128]{1,0:T(8,128)(2,1)S(1)}, bf16[816,128]{1,0:T(8,128)(2,1)S(1)}, bf16[816,128]{1,0:T(8,128)(2,1)S(1)}, bf16[816,128]{1,0:T(8,128)(2,1)}) fusion(bf16[4,816,128]{2,1,0:T(8,128)(2,1)} %attention.1), kind=kLoop, calls=%fused_computation | loop fusion | bytes 1671168 | tf_op jit(solution)/shard_map/squeeze | solution.py:321
  72.0 2.4 %collective-permute-start.12 = (bf16[816,128]{1,0:T(8,128)(2,1)S(1)}, bf16[816,128]{1,0:T(8,128)(2,1)S(1)}, u32[]{:S(2)}, u32[]{:S(2)}) collective-permute-start(bf16[816,128]{1,0:T(8,128)(2,1)S(1)} %get-tuple-element.6), channel_id=1, source_target_pairs={{0,2},{1,3},{2,0},{3,1},{4,6},{5,7},{6,4},{7,5},{8,10},{9,11},{10,... | collective-permute-start | bytes 626696 | tf_op jit(solution)/shard_map/ppermute | solution.py:236
  74.4 1.5 %collective-permute-start.13 = (bf16[816,128]{1,0:T(8,128)(2,1)S(1)}, bf16[816,128]{1,0:T(8,128)(2,1)S(1)}, u32[]{:S(2)}, u32[]{:S(2)}) collective-permute-start(bf16[816,128]{1,0:T(8,128)(2,1)S(1)} %get-tuple-element.5), channel_id=1, source_target_pairs={{0,3},{1,2},{2,1},{3,0},{4,7},{5,6},{6,5},{7,4},{8,11},{9,10},{10,... | collective-permute-start | bytes 626696 | tf_op jit(solution)/shard_map/ppermute | solution.py:236
  76.5 2.6 %gate.1.refs_4_ = f32[768,128]{1,0:T(8,128)} custom-call(bf16[128,768]{1,0:T(8,128)(2,1)} %norm.1.x_ref, bf16[768,768]{1,0:T(8,128)(2,1)} %w_ref.1), custom_call_target="tpu_custom_call" | custom-call | flops 150994944 | bytes 1179648 | tf_op jit(solution)/shard_map/gate/pallas_call | solution.py:243
  79.0 1.0 %collective-permute-done.11.refs_1_ = bf16[816,128]{1,0:T(8,128)(2,1)S(1)} collective-permute-done((bf16[816,128]{1,0:T(8,128)(2,1)S(1)}, bf16[816,128]{1,0:T(8,128)(2,1)S(1)}, u32[]{:S(2)}, u32[]{:S(2)}) %collective-permute-start.11) | collective-permute-done | bytes 208928 | tf_op jit(solution)/shard_map/ppermute | solution.py:236
  80.1 3.9 %collective-permute-done.12.refs_2_ = bf16[816,128]{1,0:T(8,128)(2,1)S(1)} collective-permute-done((bf16[816,128]{1,0:T(8,128)(2,1)S(1)}, bf16[816,128]{1,0:T(8,128)(2,1)S(1)}, u32[]{:S(2)}, u32[]{:S(2)}) %collective-permute-start.12) | collective-permute-done | bytes 208928 | tf_op jit(solution)/shard_map/ppermute | solution.py:236
  84.0 1.9 %collective-permute-done.13.refs_3_ = bf16[816,128]{1,0:T(8,128)(2,1)S(1)} collective-permute-done((bf16[816,128]{1,0:T(8,128)(2,1)S(1)}, bf16[816,128]{1,0:T(8,128)(2,1)S(1)}, u32[]{:S(2)}, u32[]{:S(2)}) %collective-permute-start.13) | collective-permute-done | bytes 208928 | tf_op jit(solution)/shard_map/ppermute | solution.py:236
  86.6 6.5 %finish.1 = bf16[128,768]{1,0:T(8,128)(2,1)} custom-call(bf16[816,128]{1,0:T(8,128)(2,1)} %get-tuple-element.8.refs_0_, bf16[816,128]{1,0:T(8,128)(2,1)} %copy-done, bf16[816,128]{1,0:T(8,128)(2,1)} %copy-done.1, bf16[816,128]{1,0:T(8,128)(2,1)} %copy-done.2, f32[768,128]{1,0:T(8,128)} %gate.1.refs_4_, bf16[128,768]{1,0:T(8,128)(2,1)} %bitcast.28, ...), custom_call_target="tpu_custom_call" | custom-call | flops 1056964608 | bytes 8257536 | tf_op jit(solution)/shard_map/finish/pallas_call | solution.py:323
  (51 shorter events, 4.2 us)
Async XLA Ops:
  0.0 36.5 %slice-start = ((bf16[768,2304]{1,0:T(8,128)(2,1)}), bf16[768,768]{1,0:T(8,128)(2,1)S(1)}, s32[]{:S(2)}) async-start(bf16[768,2304]{1,0:T(8,128)(2,1)} %refs_9_.2), calls=%async_computation | async-start | bytes 2359296 | tf_op jit(solution)/shard_map/slice | solution.py:295
  3.2 13.3 %collective-permute-start = (bf16[4,32,768]{2,1,0:T(8,128)(2,1)}, bf16[4,32,768]{2,1,0:T(8,128)(2,1)S(1)}, u32[]{:S(2)}, u32[]{:S(2)}) collective-permute-start(bf16[4,32,768]{2,1,0:T(8,128)(2,1)} %bitcast.19), channel_id=1, source_target_pairs={{0,0},{1,8},{2,16},{3,24},{4,4},{5,12},{6,20},{7,28},{8,1},{9,9},{... | collective-permute-start | bytes 589832 | tf_op jit(solution)/shard_map/ppermute | solution.py:222
  4.8 22.2 %collective-permute-start.1 = (bf16[4,32,768]{2,1,0:T(8,128)(2,1)}, bf16[4,32,768]{2,1,0:T(8,128)(2,1)S(1)}, u32[]{:S(2)}, u32[]{:S(2)}) collective-permute-start(bf16[4,32,768]{2,1,0:T(8,128)(2,1)} %bitcast.20), channel_id=1, source_target_pairs={{0,8},{1,0},{2,24},{3,16},{4,12},{5,4},{6,28},{7,20},{8,9},{9,1},{... | collective-permute-start | bytes 589832 | tf_op jit(solution)/shard_map/ppermute | solution.py:222
  9.6 17.5 %collective-permute-start.2 = (bf16[4,32,768]{2,1,0:T(8,128)(2,1)}, bf16[4,32,768]{2,1,0:T(8,128)(2,1)S(1)}, u32[]{:S(2)}, u32[]{:S(2)}) collective-permute-start(bf16[4,32,768]{2,1,0:T(8,128)(2,1)} %bitcast.21), channel_id=1, source_target_pairs={{0,16},{1,24},{2,0},{3,8},{4,20},{5,28},{6,4},{7,12},{8,17},{9,25}... | collective-permute-start | bytes 589832 | tf_op jit(solution)/shard_map/ppermute | solution.py:222
  13.1 14.1 %collective-permute-start.3 = (bf16[4,32,768]{2,1,0:T(8,128)(2,1)}, bf16[4,32,768]{2,1,0:T(8,128)(2,1)S(1)}, u32[]{:S(2)}, u32[]{:S(2)}) collective-permute-start(bf16[4,32,768]{2,1,0:T(8,128)(2,1)} %bitcast.22), channel_id=1, source_target_pairs={{0,24},{1,16},{2,8},{3,0},{4,28},{5,20},{6,12},{7,4},{8,25},{9,17}... | collective-permute-start | bytes 589832 | tf_op jit(solution)/shard_map/ppermute | solution.py:222
  15.0 12.7 %collective-permute-start.8 = (bf16[4,32,768]{2,1,0:T(8,128)(2,1)}, bf16[4,32,768]{2,1,0:T(8,128)(2,1)S(1)}, u32[]{:S(2)}, u32[]{:S(2)}) collective-permute-start(bf16[4,32,768]{2,1,0:T(8,128)(2,1)} %bitcast.23), channel_id=1, source_target_pairs={{0,1},{1,0},{2,3},{3,2},{4,5},{5,4},{6,7},{7,6},{8,9},{9,8},{10,11... | collective-permute-start | bytes 589832 | tf_op jit(solution)/shard_map/ppermute | solution.py:236
  16.5 21.4 %copy-start.3 = (bf16[4,32,768]{2,1,0:T(8,128)(2,1)}, bf16[4,32,768]{2,1,0:T(8,128)(2,1)S(1)}, u32[]{:S(2)}) copy-start(bf16[4,32,768]{2,1,0:T(8,128)(2,1)S(1)} %collective-permute-done.refs_0_) | copy-start | bytes 589828
  16.5 19.9 %collective-permute-start.9 = (bf16[4,32,768]{2,1,0:T(8,128)(2,1)}, bf16[4,32,768]{2,1,0:T(8,128)(2,1)S(1)}, u32[]{:S(2)}, u32[]{:S(2)}) collective-permute-start(bf16[4,32,768]{2,1,0:T(8,128)(2,1)} %bitcast.24), channel_id=1, source_target_pairs={{0,2},{1,3},{2,0},{3,1},{4,6},{5,7},{6,4},{7,5},{8,10},{9,11},{10,... | collective-permute-start | bytes 589832 | tf_op jit(solution)/shard_map/ppermute | solution.py:236
  27.0 10.9 %copy-start.4 = (bf16[4,32,768]{2,1,0:T(8,128)(2,1)}, bf16[4,32,768]{2,1,0:T(8,128)(2,1)S(1)}, u32[]{:S(2)}) copy-start(bf16[4,32,768]{2,1,0:T(8,128)(2,1)S(1)} %collective-permute-done.1.refs_1_) | copy-start | bytes 589828
  27.0 24.0 %collective-permute-start.10 = (bf16[4,32,768]{2,1,0:T(8,128)(2,1)}, bf16[4,32,768]{2,1,0:T(8,128)(2,1)S(1)}, u32[]{:S(2)}, u32[]{:S(2)}) collective-permute-start(bf16[4,32,768]{2,1,0:T(8,128)(2,1)} %bitcast.25), channel_id=1, source_target_pairs={{0,3},{1,2},{2,1},{3,0},{4,7},{5,6},{6,5},{7,4},{8,11},{9,10},{10,... | collective-permute-start | bytes 589832 | tf_op jit(solution)/shard_map/ppermute | solution.py:236
  27.1 10.8 %copy-start.5 = (bf16[4,32,768]{2,1,0:T(8,128)(2,1)}, bf16[4,32,768]{2,1,0:T(8,128)(2,1)S(1)}, u32[]{:S(2)}) copy-start(bf16[4,32,768]{2,1,0:T(8,128)(2,1)S(1)} %collective-permute-done.2.refs_2_) | copy-start | bytes 589828
  27.1 29.1 %collective-permute-start.4 = (bf16[4,32,768]{2,1,0:T(8,128)(2,1)S(1)}, bf16[4,32,768]{2,1,0:T(8,128)(2,1)S(1)}, u32[]{:S(2)}, u32[]{:S(2)}) collective-permute-start(bf16[4,32,768]{2,1,0:T(8,128)(2,1)S(1)} %collective-permute-done.refs_0_), channel_id=1, source_target_pairs={{0,4},{4,0},{8,12},{12,8},{16,20},{20,16},{24,28},{28,24},{1,5},{5... | collective-permute-start | bytes 589832 | tf_op jit(solution)/shard_map/ppermute | solution.py:230
  27.2 10.7 %copy-start.6 = (bf16[4,32,768]{2,1,0:T(8,128)(2,1)}, bf16[4,32,768]{2,1,0:T(8,128)(2,1)S(1)}, u32[]{:S(2)}) copy-start(bf16[4,32,768]{2,1,0:T(8,128)(2,1)S(1)} %collective-permute-done.3.refs_3_) | copy-start | bytes 589828
  27.2 29.0 %collective-permute-start.5 = (bf16[4,32,768]{2,1,0:T(8,128)(2,1)S(1)}, bf16[4,32,768]{2,1,0:T(8,128)(2,1)S(1)}, u32[]{:S(2)}, u32[]{:S(2)}) collective-permute-start(bf16[4,32,768]{2,1,0:T(8,128)(2,1)S(1)} %collective-permute-done.1.refs_1_), channel_id=1, source_target_pairs={{0,4},{4,0},{8,12},{12,8},{16,20},{20,16},{24,28},{28,24},{1,5},{5... | collective-permute-start | bytes 589832 | tf_op jit(solution)/shard_map/ppermute | solution.py:230
  27.7 10.2 %copy-start.7 = (bf16[4,32,768]{2,1,0:T(8,128)(2,1)}, bf16[4,32,768]{2,1,0:T(8,128)(2,1)S(1)}, u32[]{:S(2)}) copy-start(bf16[4,32,768]{2,1,0:T(8,128)(2,1)S(1)} %collective-permute-done.8.refs_1_) | copy-start | bytes 589828
  27.7 28.5 %collective-permute-start.6 = (bf16[4,32,768]{2,1,0:T(8,128)(2,1)S(1)}, bf16[4,32,768]{2,1,0:T(8,128)(2,1)S(1)}, u32[]{:S(2)}, u32[]{:S(2)}) collective-permute-start(bf16[4,32,768]{2,1,0:T(8,128)(2,1)S(1)} %collective-permute-done.2.refs_2_), channel_id=1, source_target_pairs={{0,4},{4,0},{8,12},{12,8},{16,20},{20,16},{24,28},{28,24},{1,5},{5... | collective-permute-start | bytes 589832 | tf_op jit(solution)/shard_map/ppermute | solution.py:230
  36.4 1.5 %copy-start.9 = (bf16[4,32,768]{2,1,0:T(8,128)(2,1)}, bf16[4,32,768]{2,1,0:T(8,128)(2,1)S(1)}, u32[]{:S(2)}) copy-start(bf16[4,32,768]{2,1,0:T(8,128)(2,1)S(1)} %collective-permute-done.9.refs_2_) | copy-start | bytes 589828
  36.4 19.9 %collective-permute-start.7 = (bf16[4,32,768]{2,1,0:T(8,128)(2,1)S(1)}, bf16[4,32,768]{2,1,0:T(8,128)(2,1)S(1)}, u32[]{:S(2)}, u32[]{:S(2)}) collective-permute-start(bf16[4,32,768]{2,1,0:T(8,128)(2,1)S(1)} %collective-permute-done.3.refs_3_), channel_id=1, source_target_pairs={{0,4},{4,0},{8,12},{12,8},{16,20},{20,16},{24,28},{28,24},{1,5},{5... | collective-permute-start | bytes 589832 | tf_op jit(solution)/shard_map/ppermute | solution.py:230
  57.1 18.8 %copy-start.14 = (f32[768]{0:T(1024)S(1)}, f32[768]{0:T(1024)}, u32[]{:S(2)}) copy-start(f32[768]{0:T(1024)} %param.19) | copy-start | bytes 9220
  72.0 8.0 %collective-permute-start.11 = (bf16[816,128]{1,0:T(8,128)(2,1)S(1)}, bf16[816,128]{1,0:T(8,128)(2,1)S(1)}, u32[]{:S(2)}, u32[]{:S(2)}) collective-permute-start(bf16[816,128]{1,0:T(8,128)(2,1)S(1)} %get-tuple-element.7), channel_id=1, source_target_pairs={{0,1},{1,0},{2,3},{3,2},{4,5},{5,4},{6,7},{7,6},{8,9},{9,8},{10,11... | collective-permute-start | bytes 626696 | tf_op jit(solution)/shard_map/ppermute | solution.py:236
  72.0 12.0 %collective-permute-start.12 = (bf16[816,128]{1,0:T(8,128)(2,1)S(1)}, bf16[816,128]{1,0:T(8,128)(2,1)S(1)}, u32[]{:S(2)}, u32[]{:S(2)}) collective-permute-start(bf16[816,128]{1,0:T(8,128)(2,1)S(1)} %get-tuple-element.6), channel_id=1, source_target_pairs={{0,2},{1,3},{2,0},{3,1},{4,6},{5,7},{6,4},{7,5},{8,10},{9,11},{10,... | collective-permute-start | bytes 626696 | tf_op jit(solution)/shard_map/ppermute | solution.py:236
  74.4 11.5 %collective-permute-start.13 = (bf16[816,128]{1,0:T(8,128)(2,1)S(1)}, bf16[816,128]{1,0:T(8,128)(2,1)S(1)}, u32[]{:S(2)}, u32[]{:S(2)}) collective-permute-start(bf16[816,128]{1,0:T(8,128)(2,1)S(1)} %get-tuple-element.5), channel_id=1, source_target_pairs={{0,3},{1,2},{2,1},{3,0},{4,7},{5,6},{6,5},{7,4},{8,11},{9,10},{10,... | collective-permute-start | bytes 626696 | tf_op jit(solution)/shard_map/ppermute | solution.py:236
  80.1 5.8 %copy-start = (bf16[816,128]{1,0:T(8,128)(2,1)}, bf16[816,128]{1,0:T(8,128)(2,1)S(1)}, u32[]{:S(2)}) copy-start(bf16[816,128]{1,0:T(8,128)(2,1)S(1)} %collective-permute-done.11.refs_1_) | copy-start | bytes 626692
  84.0 1.9 %copy-start.1 = (bf16[816,128]{1,0:T(8,128)(2,1)}, bf16[816,128]{1,0:T(8,128)(2,1)S(1)}, u32[]{:S(2)}) copy-start(bf16[816,128]{1,0:T(8,128)(2,1)S(1)} %collective-permute-done.12.refs_2_) | copy-start | bytes 626692
  (6 other events, 4.4 us)
